TPU v7x, 128 devices: a whole 4x4x4 slice. The times are simulated.
128 devices in a mesh: row: 8 (over z, core), col: 16 (over y, x).
Axes of the slice: x: 4, y: 4, z: 4, core: 2. Of those that a mesh axis runs over, the one named last changes fastest.
Arguments:
- fock: bfloat16 [18432, 18432], P('row', 'col'), may hold values from -6 to 6
- intersection: bfloat16 [18432, 18432], P('row', 'col'), may hold values from -6 to 6
- tile_mask: int32 [2, 144, 144], P(None, 'row', 'col'), may hold values 0 or 1
- coefficients: bfloat16 [256, 7, 20, 128], P(('row', 'col')), may hold values from -0.5 to 0.5
- domains: int32 [256, 7], P(('row', 'col')), may hold values from 0 to 143, all different within a row; in each aligned block of 32 rows (0 to 31, 32 to 63, ...) at most 2 rows name the same one
- neighbours: int32 [256, 2], P(('row', 'col')), may hold values from 0 to 255, all different within a row
- amplitudes: float32 [256, 20, 20], P(('row', 'col')), may hold values from -0.18 to 0.18
Outputs:
- projected: float32 [256, 20, 20], P(('row', 'col'))
Inputs may be any that keep to these rules, and one draw needn't show every extreme that they name: `domains`: each pair names 7 different tiles; among the 32 pairs of one row index (an aligned block of pairs) no tile is named by more than 2 slots. `neighbours`: each pair names 2 different pairs.
All inputs are finite; a program needn't handle non-finite values. No bound on the sum of `tile_mask` on one device may be relied on, other than what follows from the above.
Results may differ from a plain program's by a relative error of at most 0.0041.
Values may be sent and summed in bfloat16 or wider, within the bound.
A program may use at most 256 MiB of HBM per device.

v0:
```python
import jax
import jax.numpy as jnp
from jax import lax
from jax.sharding import PartitionSpec as P

HIGH = lax.Precision.HIGHEST


def in_one_piece(arrays, axis, dim, along):
    both = jnp.concatenate(arrays, axis=along)
    whole, at, done = (lax.all_gather(both, axis, axis=dim, tiled=True), 0, [])
    for a in arrays:
        done.append(lax.slice_in_dim(whole, at, at + a.shape[along], axis=along))
        at += a.shape[along]
    return tuple(done)


def split_up(x, dim, length):
    dims = x.shape
    tiles = x.reshape(*dims[:dim], length, dims[dim] // length, *dims[dim + 1 :])
    return jnp.moveaxis(tiles, dim, 0)


def sent_and_summed(x, axis, dim):
    tiles = split_up(x, dim, lax.axis_size(axis))
    arrived = lax.all_to_all(tiles, axis, split_axis=0, concat_axis=0, tiled=True)
    return arrived.sum(axis=0)


def bucket_slots(coeffs, tiles, base_pair, first_tile, tile_count, capacity):
    group_size, per_pair = tiles.shape
    slot_count = group_size * per_pair
    flat_tiles = tiles.reshape(slot_count)
    position = jnp.arange(slot_count, dtype=jnp.int32)
    pair_owner = base_pair + position // per_pair
    earlier = (flat_tiles[:, None] == flat_tiles[None, :]) & (position[None, :] < position[:, None])
    slot_rank = jnp.sum(earlier.astype(jnp.int32), axis=1)
    wanted = first_tile + jnp.arange(tile_count, dtype=jnp.int32)
    levels = jnp.arange(capacity, dtype=jnp.int32)
    matches = (flat_tiles[None, None, :] == wanted[:, None, None]) & (
        slot_rank[None, None, :] == levels[None, :, None]
    )
    present = jnp.any(matches, axis=2)
    source = jnp.sum(matches.astype(jnp.int32) * position[None, None, :], axis=2)
    flat_coeffs = coeffs.reshape((slot_count,) + coeffs.shape[2:])
    blocks = jnp.take(flat_coeffs, source, axis=0)
    blocks = jnp.where(present[:, :, None, None], blocks, jnp.zeros((), blocks.dtype))
    owners = jnp.where(present, jnp.take(pair_owner, source), -1)
    return (blocks, owners)


def shards(fock, intersection, tile_mask, coefficients, domains, neighbours, amplitudes):
    row_count = lax.axis_size("row")
    col_count = lax.axis_size("col")
    row_index = lax.axis_index("row")
    col_index = lax.axis_index("col")
    pair_dev, per_pair, pno_count, tile_size = coefficients.shape
    link_count = neighbours.shape[1]
    tile_rows = fock.shape[0] // tile_size
    tile_cols = fock.shape[1] // tile_size
    capacity = max(2, pair_dev)
    group_size = pair_dev * col_count
    width = fock.shape[1]
    group_coeffs, group_tiles, group_links = (
        lax.all_gather(coefficients, "col", axis=0, tiled=True),
        *in_one_piece((domains, neighbours), "col", 0, 1),
    )

    def rows_of(coeffs, tiles, base_pair):
        return bucket_slots(coeffs, tiles, base_pair, row_index * tile_rows, tile_rows, capacity)

    def cols_of(coeffs, tiles, base_pair):
        return bucket_slots(coeffs, tiles, base_pair, col_index * tile_cols, tile_cols, capacity)

    all_coeffs, all_tiles, all_links = (
        lax.all_gather(group_coeffs, "row", axis=0, tiled=True),
        lax.all_gather(group_tiles, "row", axis=0, tiled=True),
        lax.all_gather(group_links, "row", axis=0, tiled=True),
    )
    grouped_coeffs = all_coeffs.reshape((row_count, group_size) + all_coeffs.shape[1:])
    grouped_tiles = all_tiles.reshape(row_count, group_size, per_pair)
    bases = jnp.arange(row_count, dtype=jnp.int32) * group_size
    row_blocks, row_owners = jax.vmap(rows_of)(grouped_coeffs, grouped_tiles, bases)
    col_blocks, col_owners = jax.vmap(cols_of)(grouped_coeffs, grouped_tiles, bases)

    def masked(matrix, flags):
        tiled = matrix.reshape(tile_rows, tile_size, tile_cols, tile_size)
        return (tiled * flags.astype(matrix.dtype)[:, None, :, None]).reshape(matrix.shape)

    operator = jnp.concatenate(
        [masked(fock, tile_mask[0]), masked(intersection, tile_mask[1])], axis=1
    )
    operator = operator.reshape(tile_rows, tile_size, 2 * width)
    link_groups = all_links.reshape(row_count, group_size, link_count)
    group_bases = jnp.arange(row_count, dtype=jnp.int32) * group_size

    def one_group(inputs):
        blocks, owners, links_here, base_pair = inputs
        parts = jnp.einsum("tmak,tkw->tmaw", blocks, operator, preferred_element_type=jnp.float32)
        members = base_pair + jnp.arange(group_size, dtype=jnp.int32)
        flat_owners = owners.reshape(-1)
        bucket_count = flat_owners.shape[0]
        flat_parts = parts.reshape(bucket_count, pno_count, 2 * width)
        hits = flat_owners[None, :] == members[:, None]
        order = jnp.cumsum(hits.astype(jnp.int32), axis=1) - 1
        spots = jnp.arange(bucket_count, dtype=jnp.int32)
        total = jnp.zeros((group_size, pno_count, 2 * width), jnp.float32)
        for slot in range(per_pair):
            pick = hits & (order == slot)
            found = jnp.any(pick, axis=1)
            where_at = jnp.sum(pick.astype(jnp.int32) * spots[None, :], axis=1)
            picked = jnp.take(flat_parts, where_at, axis=0)
            total = total + jnp.where(found[:, None, None], picked, jnp.zeros((), jnp.float32))
        left = total.astype(jnp.bfloat16)
        left = left.reshape(group_size, pno_count, 2, tile_cols, tile_size)
        chosen = (col_owners[None, None] == links_here[:, :, None, None, None]).astype(jnp.bfloat16)
        partner = jnp.einsum(
            "qngtm,gtmbk->qntbk", chosen, col_blocks, preferred_element_type=jnp.float32
        ).astype(jnp.bfloat16)
        return jnp.einsum("qamtk,qntbk->qnmab", left, partner, preferred_element_type=jnp.float32)

    terms = lax.map(one_group, (row_blocks, row_owners, link_groups, group_bases))
    flat_terms = terms.reshape(row_count * group_size, -1)
    sectioned = flat_terms.reshape(row_count, col_count, pair_dev, -1)
    sectioned = sent_and_summed(sectioned, "col", 1)
    summed = sent_and_summed(sectioned, "row", 0)
    summed = summed.reshape(pair_dev, link_count, 2, pno_count, pno_count)
    every_amp = lax.all_gather(amplitudes, ("row", "col"), axis=0, tiled=True)
    nearby = jnp.take(every_amp, neighbours, axis=0)
    fock_part = summed[:, :, 0]
    over_part = summed[:, :, 1]
    first = jnp.einsum("pnab,pnbc,pndc->pad", over_part, nearby, fock_part, precision=HIGH)
    second = jnp.einsum("pnab,pnbc,pndc->pad", fock_part, nearby, over_part, precision=HIGH)
    return first + second


def solution(mesh):
    placed = (
        P("row", "col"),
        P("row", "col"),
        P(None, "row", "col"),
        P(("row", "col"), None, None, None),
        P(("row", "col"), None),
        P(("row", "col"), None),
        P(("row", "col"), None, None),
    )
    return jax.shard_map(
        shards, mesh=mesh, in_specs=placed, out_specs=P(("row", "col"), None, None), check_vma=False
    )
```

profile of v0, /device:TPU:1, one launch (start us, length us, event | category | flops | bytes accessed | tf_op | source)
XLA Modules:
  0.0 1135.7 jit_solution(11759695750382023470)
XLA Ops:
  8.1 45.8 %all-gather.6.cloned.1.call-done = bf16[32,7,20,128]{3,1,2,0:T(8,128)(2,1)} async-done(((bf16[2,7,20,128]{3,1,2,0:T(8,128)(2,1)}), bf16[32,7,20,128]{3,1,2,0:T(8,128)(2,1)}) %all-gather.6.cloned.1.call-update) | async-done | bytes 1146896 | tf_op jit(solution)/shard_map/all_gather | solution.py:65
  57.5 17.6 %all-gather = s32[16,2,9]{2,1,0:T(2,128)S(1)} all-gather(s32[1,2,9]{2,1,0:T(2,128)S(1)} %add_bitcast_fusion), channel_id=1, replica_groups=mesh['row'=8,'col'=16] {'col'}, dimensions={0}, use_global_device_ids=true | all-gather | bytes 1224 | tf_op jit(solution)/shard_map/all_gather | solution.py:11
  75.3 21.1 %all-gather.1 = s32[8,32,7]{1,2,0:T(8,128)S(1)} all-gather(s32[1,32,7]{1,2,0:T(8,128)S(1)} %bitcast.147), channel_id=1, replica_groups=mesh['row'=8,'col'=16] {'row'}, dimensions={0}, use_global_device_ids=true | all-gather | bytes 8064 | tf_op jit(solution)/shard_map/all_gather | solution.py:77
  107.7 8.5 copy.140
  122.7 8.6 copy.141
  131.3 8.5 copy.142
  146.3 8.6 copy.143
  154.9 11.2 all-gather.2
  166.6 9.3 pad_maximum_fusion
  175.8 13.8 %copy.171 = bf16[256,7,20,128]{3,2,1,0:T(8,128)(2,1)} copy(bf16[256,7,20,128]{3,0,2,1:T(8,128)(2,1)} %all-gather.8.cloned.1.call-done) | data formatting | bytes 18350080 | tf_op jit(solution)/shard_map/vmap()/reshape;reshape | solution.py:45
  189.6 7.2 gather_fusion.11
  206.1 806.4 %while.12 = (s32[]{:T(128)}, f32[8,32,2,2,20,20]{5,4,3,2,0,1:T(8,128)}, s32[8,9,2]{0,2,1:T(2,128)S(1)}, s32[8,32,2]{1,2,0:T(2,128)}, bf16[8,9,2,20,128]{4,0,2,3,...) while((s32[]{:T(128)}, ...), condition=%wide.region_21.23_spmd, body=%wide.region_5.22_spmd.sunk | while | flops 622367552 | bytes 162233904 | solution.py:122
  210.4 8.9 fusion.72
  219.3 7.1 gather_fusion.1
  226.7 7.2 gather_fusion.2
  233.8 7.1 gather_fusion.3
  241.2 7.1 gather_fusion.4
  255.4 7.1 gather_fusion
  271.5 18.9 %fusion.74 = bf16[32,20,2304]{2,1,0:T(8,128)(2,1)S(1)} fusion(f32[32,20,2304]{2,1,0:T(8,128)} %gather_fusion, f32[32,20,2304]{2,1,0:T(8,128)} %gather_fusion.1, f32[32,20,2304]{2,1,0:T(8,128)} %gather_fusion.2, f32[32,20,2304]{2,1,0:T(8,128)} %gather_fusion.3, f32[32,20,2304]{2,1,0:T(8,128)} %gather_fusion.4, f32[32,20,2304]{2,1,0:T(8,128)} %gather_fusion.5, ...), kind=kLoop, calls=%fused_computation.16.clone.1 | loop fusion | flops 30965760 | bytes 44237248 | tf_op jit(solution)/shard_map/while/body/eval_jaxpr/convert_element_type | solution.py:114
  311.2 8.9 fusion.72
  327.4 7.2 gather_fusion.2
  334.5 7.1 gather_fusion.3
  341.9 7.1 gather_fusion.4
  356.2 7.1 gather_fusion
  372.2 18.9 %fusion.74 = bf16[32,20,2304]{2,1,0:T(8,128)(2,1)S(1)} fusion(f32[32,20,2304]{2,1,0:T(8,128)} %gather_fusion, f32[32,20,2304]{2,1,0:T(8,128)} %gather_fusion.1, f32[32,20,2304]{2,1,0:T(8,128)} %gather_fusion.2, f32[32,20,2304]{2,1,0:T(8,128)} %gather_fusion.3, f32[32,20,2304]{2,1,0:T(8,128)} %gather_fusion.4, f32[32,20,2304]{2,1,0:T(8,128)} %gather_fusion.5, ...), kind=kLoop, calls=%fused_computation.16.clone.1 | loop fusion | flops 30965760 | bytes 44237248 | tf_op jit(solution)/shard_map/while/body/eval_jaxpr/convert_element_type | solution.py:114
  411.9 8.9 fusion.72
  420.8 7.1 gather_fusion.1
  428.1 7.2 gather_fusion.2
  435.3 7.1 gather_fusion.3
  442.6 7.1 gather_fusion.4
  456.9 7.1 gather_fusion
  472.9 18.9 %fusion.74 = bf16[32,20,2304]{2,1,0:T(8,128)(2,1)S(1)} fusion(f32[32,20,2304]{2,1,0:T(8,128)} %gather_fusion, f32[32,20,2304]{2,1,0:T(8,128)} %gather_fusion.1, f32[32,20,2304]{2,1,0:T(8,128)} %gather_fusion.2, f32[32,20,2304]{2,1,0:T(8,128)} %gather_fusion.3, f32[32,20,2304]{2,1,0:T(8,128)} %gather_fusion.4, f32[32,20,2304]{2,1,0:T(8,128)} %gather_fusion.5, ...), kind=kLoop, calls=%fused_computation.16.clone.1 | loop fusion | flops 30965760 | bytes 44237248 | tf_op jit(solution)/shard_map/while/body/eval_jaxpr/convert_element_type | solution.py:114
  512.7 8.9 fusion.72
  528.9 7.2 gather_fusion.2
  536.0 7.1 gather_fusion.3
  543.4 7.1 gather_fusion.4
  557.7 7.1 gather_fusion
  573.7 18.9 %fusion.74 = bf16[32,20,2304]{2,1,0:T(8,128)(2,1)S(1)} fusion(f32[32,20,2304]{2,1,0:T(8,128)} %gather_fusion, f32[32,20,2304]{2,1,0:T(8,128)} %gather_fusion.1, f32[32,20,2304]{2,1,0:T(8,128)} %gather_fusion.2, f32[32,20,2304]{2,1,0:T(8,128)} %gather_fusion.3, f32[32,20,2304]{2,1,0:T(8,128)} %gather_fusion.4, f32[32,20,2304]{2,1,0:T(8,128)} %gather_fusion.5, ...), kind=kLoop, calls=%fused_computation.16.clone.1 | loop fusion | flops 30965760 | bytes 44237248 | tf_op jit(solution)/shard_map/while/body/eval_jaxpr/convert_element_type | solution.py:114
  613.4 8.9 fusion.72
  629.6 7.2 gather_fusion.2
  636.8 7.1 gather_fusion.3
  644.2 7.1 gather_fusion.4
  658.4 7.1 gather_fusion
  674.4 18.9 %fusion.74 = bf16[32,20,2304]{2,1,0:T(8,128)(2,1)S(1)} fusion(f32[32,20,2304]{2,1,0:T(8,128)} %gather_fusion, f32[32,20,2304]{2,1,0:T(8,128)} %gather_fusion.1, f32[32,20,2304]{2,1,0:T(8,128)} %gather_fusion.2, f32[32,20,2304]{2,1,0:T(8,128)} %gather_fusion.3, f32[32,20,2304]{2,1,0:T(8,128)} %gather_fusion.4, f32[32,20,2304]{2,1,0:T(8,128)} %gather_fusion.5, ...), kind=kLoop, calls=%fused_computation.16.clone.1 | loop fusion | flops 30965760 | bytes 44237248 | tf_op jit(solution)/shard_map/while/body/eval_jaxpr/convert_element_type | solution.py:114
  714.2 8.9 fusion.72
  730.4 7.2 gather_fusion.2
  737.5 7.1 gather_fusion.3
  744.9 7.1 gather_fusion.4
  759.2 7.1 gather_fusion
  775.2 18.9 %fusion.74 = bf16[32,20,2304]{2,1,0:T(8,128)(2,1)S(1)} fusion(f32[32,20,2304]{2,1,0:T(8,128)} %gather_fusion, f32[32,20,2304]{2,1,0:T(8,128)} %gather_fusion.1, f32[32,20,2304]{2,1,0:T(8,128)} %gather_fusion.2, f32[32,20,2304]{2,1,0:T(8,128)} %gather_fusion.3, f32[32,20,2304]{2,1,0:T(8,128)} %gather_fusion.4, f32[32,20,2304]{2,1,0:T(8,128)} %gather_fusion.5, ...), kind=kLoop, calls=%fused_computation.16.clone.1 | loop fusion | flops 30965760 | bytes 44237248 | tf_op jit(solution)/shard_map/while/body/eval_jaxpr/convert_element_type | solution.py:114
  814.9 8.9 fusion.72
  831.1 7.2 gather_fusion.2
  838.3 7.1 gather_fusion.3
  845.7 7.1 gather_fusion.4
  859.9 7.1 gather_fusion
  875.9 18.9 %fusion.74 = bf16[32,20,2304]{2,1,0:T(8,128)(2,1)S(1)} fusion(f32[32,20,2304]{2,1,0:T(8,128)} %gather_fusion, f32[32,20,2304]{2,1,0:T(8,128)} %gather_fusion.1, f32[32,20,2304]{2,1,0:T(8,128)} %gather_fusion.2, f32[32,20,2304]{2,1,0:T(8,128)} %gather_fusion.3, f32[32,20,2304]{2,1,0:T(8,128)} %gather_fusion.4, f32[32,20,2304]{2,1,0:T(8,128)} %gather_fusion.5, ...), kind=kLoop, calls=%fused_computation.16.clone.1 | loop fusion | flops 30965760 | bytes 44237248 | tf_op jit(solution)/shard_map/while/body/eval_jaxpr/convert_element_type | solution.py:114
  915.7 8.9 fusion.72
  931.9 7.2 gather_fusion.2
  939.1 7.1 gather_fusion.3
  946.4 7.1 gather_fusion.4
  960.7 7.1 gather_fusion
  976.7 18.9 %fusion.74 = bf16[32,20,2304]{2,1,0:T(8,128)(2,1)S(1)} fusion(f32[32,20,2304]{2,1,0:T(8,128)} %gather_fusion, f32[32,20,2304]{2,1,0:T(8,128)} %gather_fusion.1, f32[32,20,2304]{2,1,0:T(8,128)} %gather_fusion.2, f32[32,20,2304]{2,1,0:T(8,128)} %gather_fusion.3, f32[32,20,2304]{2,1,0:T(8,128)} %gather_fusion.4, f32[32,20,2304]{2,1,0:T(8,128)} %gather_fusion.5, ...), kind=kLoop, calls=%fused_computation.16.clone.1 | loop fusion | flops 30965760 | bytes 44237248 | tf_op jit(solution)/shard_map/while/body/eval_jaxpr/convert_element_type | solution.py:114
  1012.6 9.4 reshape_reshape_reshape.3
  1025.9 89.9 %all_gather.18 = f32[256,20,20]{2,1,0:T(8,128)} all-gather(f32[2,20,20]{2,1,0:T(8,128)S(1)} %copy.122), channel_id=1, replica_groups=mesh['row'=8,'col'=16] {'row','col'}, dimensions={0}, use_global_device_ids=true | all-gather | bytes 412800 | tf_op jit(solution)/shard_map/all_gather | solution.py:128
  (382 shorter events, 395.8 us)
Async XLA Ops:
  6.5 47.4 %all-gather.6.cloned.1.call-start = ((), (), s32[]{:S(2)}) async-start(), calls=%async_computation.2 | async-start | bytes 1392640 | tf_op jit(solution)/shard_map/all_gather | solution.py:65
  8.1 167.7 %all-gather.8.cloned.1.call-start = ((), (), s32[]{:S(2)}) async-start(), calls=%async_computation.3 | async-start | bytes 10321920 | tf_op jit(solution)/shard_map/all_gather | solution.py:76
  106.6 9.7 copy-start.1
  1012.6 13.2 %copy-start = (f32[2,20,20]{2,0,1:T(2,128)S(1)}, f32[2,20,20]{2,0,1:T(2,128)}, u32[]{:S(2)}) copy-start(f32[2,20,20]{2,0,1:T(2,128)} %param.17) | copy-start | bytes 9604
  1012.6 13.2 %copy-start.2 = (s32[2,2]{1,0:T(2,128)S(1)}, s32[2,2]{1,0:T(2,128)}, u32[]{:S(2)}) copy-start(s32[2,2]{1,0:T(2,128)} %param.16) | copy-start | bytes 52
  1022.0 93.9 %all-to-all-start = ((f32[16,8,1,2,1600]{4,1,3,2,0:T(8,128)}), f32[16,8,1,2,1600]{4,1,3,2,0:T(8,128)S(1)}, u32[]{:S(2)}, u32[]{:S(2)}) async-start(f32[16,8,1,2,1600]{4,1,3,2,0:T(8,128)} %bitcast.33), calls=%async_computation | async-start | bytes 3407872 | tf_op jit(solution)/shard_map/all_to_all | solution.py:26
  1116.7 10.0 all-to-all-start.1
Sparse Core Ops, SparseCore 0:
  9.5 44.3 all-gather.5
  56.9 55.0 all-gather.7
where the time goes:
time: 1150 us; the launch traced here: 1140 us
  local copies, waits for them, and re-layouts  564 us (49%)
  other arithmetic  215 us (19%)
  matrix products  144 us (13%)
  blocking collectives  140 us (12%)
  waiting for transfers between devices  48.2 us (4%)
  between operations  14.2 us (1%)
    gather x56, local copies, waits for them, and re-layouts, one_group(): picked = jnp.take(flat_parts, where_at, axis=0)  398 us
    convert_element_type x8, other arithmetic, one_group(): left = total.astype(jnp.bfloat16)  151 us
    all_gather x1, blocking collectives, shards(): every_amp = lax.all_gather(amplitudes, ('row', 'col'), axis=0, tiled=True)  89.9 us
    dot_general x8, matrix products, one_group(): jnp.einsum('tmak,tkw->tmaw', blocks, operator, preferred_element_type=jnp...  70.9 us
    dot_general x8, matrix products, one_group(): jnp.einsum('qamtk,qntbk->qnmab', left, partner, preferred_element_type=jn...  54 us
    all_gather x1, waiting for transfers between devices, shards(): lax.all_gather(coefficients, 'col', axis=0, tiled=True)  45.8 us
    reshape x8, local copies, waits for them, and re-layouts, one_group(): left = left.reshape(group_size, pno_count, 2, tile_cols, tile_size)  38.2 us
  transfers between devices with their start and end apart: 4, of which 2 were waited for; matrix products, arithmetic and copies ran while one was open for 6% of the time, Pallas kernels for 0%

commit v1 on v0

v1 whole, which is shorter than its diff:
```python
import functools
import jax
import jax.numpy as jnp
from jax import lax
from jax.experimental import pallas as pl
from jax.experimental.pallas import tpu as pltpu
from jax.sharding import PartitionSpec as P

HIGH = lax.Precision.HIGHEST
UNROLL = 4
LANES = 32


def slot_tables(tiles, first, count):
    packed = jnp.zeros(tiles.shape[:1], jnp.int32)
    seen = jnp.zeros(tiles.shape[:1], jnp.int32)
    for s in range(tiles.shape[1]):
        here = ((tiles[:, s] >= first) & (tiles[:, s] < first + count)).astype(jnp.int32)
        packed = packed + here * (s << (3 * seen))
        seen = seen + here
    return packed, seen


def pair_blocks_kernel(
    dims, dom, nb, rowp, colp, work, mask, c_hbm, f_hbm, s_hbm, g_ref, cv, fv, sv, l1, l2, sems
):
    pairs, slots, rows, tile, tile_rows, tile_cols = dims
    copies = (
        pltpu.make_async_copy(c_hbm, cv, sems.at[0]),
        pltpu.make_async_copy(f_hbm, fv, sems.at[1]),
        pltpu.make_async_copy(s_hbm, sv, sems.at[2]),
    )
    for c in copies:
        c.start()
    row0 = lax.axis_index("row") * tile_rows
    col0 = lax.axis_index("col") * tile_cols
    g_ref[...] = jnp.zeros_like(g_ref)
    cells = tile_rows * tile_cols

    def one_pair(d, i, counts):
        p = 2 * d + i
        w = work[p]

        def busy(counts):
            out = list(counts)
            packed_rows = rowp[p]
            n_rows = w & 7
            for n in range(2):
                q = 2 * i + n
                k = nb[2 * p + n]
                packed_cols = colp[k]
                n_cols = (w >> (3 + 3 * n)) & 7

                def by_row(x, cnt, k=k, packed_cols=packed_cols, n_cols=n_cols, q=q):
                    sa = p * slots + ((packed_rows >> (3 * x)) & 7)
                    a = dom[sa] - row0

                    def by_col(y, cnt):
                        sb = k * slots + ((packed_cols >> (3 * y)) & 7)
                        b = dom[sb] - col0
                        cell = a * tile_cols + b
                        m0 = mask[cell]
                        m1 = mask[cells + cell]
                        l1[q, cnt] = sa | (sb << 11) | (a << 22) | (b << 27)
                        l2[q, cnt] = d | (m0 << 8) | (m1 << 9)
                        return cnt + (m0 | m1)

                    return lax.fori_loop(0, n_cols, by_col, cnt)

                out[q] = lax.fori_loop(0, n_rows, by_row, out[q])
            return tuple(out)

        return lax.cond(w != 0, busy, lambda c: c, counts)

    def per_device(d, counts):
        counts = one_pair(d, 0, counts)
        return one_pair(d, 1, counts)

    zero = jnp.int32(0)
    counts = lax.fori_loop(0, pairs // 2, per_device, (zero, zero, zero, zero))
    for q in range(4):
        for x in range(UNROLL):
            l1[q, counts[q] + x] = zero
            l2[q, counts[q] + x] = zero
    for c in copies:
        c.wait()

    def product(q, i):
        w1 = l1[q, i]
        w2 = l2[q, i]
        sa = w1 & 2047
        sb = (w1 >> 11) & 2047
        a = pl.multiple_of(((w1 >> 22) & 31) * tile, tile)
        b = pl.multiple_of(((w1 >> 27) & 15) * tile, tile)
        both = jnp.concatenate([fv[pl.ds(a, tile), pl.ds(b, tile)], sv[pl.ds(a, tile), pl.ds(b, tile)]], axis=1)
        t = jnp.dot(cv[sa], both, preferred_element_type=jnp.float32)
        m0 = ((w2 >> 8) & 1).astype(jnp.float32)
        m1 = ((w2 >> 9) & 1).astype(jnp.float32)
        partner = cv[sb]
        dn = (((1,), (1,)), ((), ()))
        uf = lax.dot_general((t[:, :tile] * m0).astype(jnp.bfloat16), partner, dn, preferred_element_type=jnp.float32)
        us = lax.dot_general((t[:, tile:] * m1).astype(jnp.bfloat16), partner, dn, preferred_element_type=jnp.float32)
        return w2 & 255, uf, us

    for q in range(4):
        lo = q * LANES

        def body(it, carry, q=q, lo=lo):
            done = [product(q, it * UNROLL + x) for x in range(UNROLL)]
            for d, uf, us in done:
                g_ref[2 * d, :rows, lo : lo + rows] += uf
                g_ref[2 * d + 1, :rows, lo : lo + rows] += us
            return carry

        lax.fori_loop(0, (counts[q] + UNROLL - 1) // UNROLL, body, 0)


def shards(fock, intersection, tile_mask, coefficients, domains, neighbours, amplitudes):
    pair_dev, slots, rows, tile = coefficients.shape
    tile_rows, tile_cols = fock.shape[0] // tile, fock.shape[1] // tile
    n_dev = lax.axis_size("row") * lax.axis_size("col")
    pairs = pair_dev * n_dev
    both = ("row", "col")
    c_all = lax.all_gather(coefficients.reshape(pair_dev * slots, rows, tile), both, axis=0, tiled=True)
    tabs = lax.all_gather(jnp.concatenate([domains, neighbours], axis=1), both, axis=0, tiled=True)
    dom, nb = tabs[:, :slots], tabs[:, slots:]
    rowp, rown = slot_tables(dom, lax.axis_index("row") * tile_rows, tile_rows)
    colp, coln = slot_tables(dom, lax.axis_index("col") * tile_cols, tile_cols)
    linked = jnp.take(coln, nb.reshape(-1), axis=0).reshape(pairs, 2)
    work = rown | (linked[:, 0] << 3) | (linked[:, 1] << 6)
    work = jnp.where((rown > 0) & (linked.sum(axis=1) > 0), work, 0)
    smem = pl.BlockSpec(memory_space=pltpu.SMEM)
    anys = pl.BlockSpec(memory_space=pl.ANY)
    cap = tile_rows * 2 * (pairs // 32) // 2 * slots + 2 * UNROLL
    g = pl.pallas_call(
        functools.partial(pair_blocks_kernel, (pairs, slots, rows, tile, tile_rows, tile_cols)),
        out_shape=jax.ShapeDtypeStruct((2 * n_dev, 24, 128), jnp.float32),
        in_specs=[smem] * 6 + [anys] * 3,
        out_specs=pl.BlockSpec(memory_space=pltpu.VMEM),
        scratch_shapes=[
            pltpu.VMEM((pairs * slots, rows, tile), jnp.bfloat16),
            pltpu.VMEM(fock.shape, jnp.bfloat16),
            pltpu.VMEM(fock.shape, jnp.bfloat16),
            pltpu.SMEM((4, 2048), jnp.int32),
            pltpu.SMEM((4, 2048), jnp.int32),
            pltpu.SemaphoreType.DMA((3,)),
        ],
        compiler_params=pltpu.CompilerParams(vmem_limit_bytes=56 * 2**20),
    )(dom.reshape(-1), nb.reshape(-1), rowp, colp, work, tile_mask.reshape(-1), c_all, fock, intersection)
    g = g.reshape(lax.axis_size("row"), lax.axis_size("col"), 2, 24, 128)
    g = lax.all_to_all(g, "col", split_axis=1, concat_axis=1, tiled=True).sum(axis=1)
    g = lax.all_to_all(g, "row", split_axis=0, concat_axis=0, tiled=True).sum(axis=0)
    blocks = g[:, :rows].reshape(2, rows, 2, 2, LANES)[..., :rows]
    fock_part = jnp.transpose(blocks[0], (1, 2, 0, 3))
    over_part = jnp.transpose(blocks[1], (1, 2, 0, 3))
    every_amp = lax.all_gather(amplitudes, both, axis=0, tiled=True)
    nearby = jnp.take(every_amp, neighbours, axis=0)
    first = jnp.einsum("pnab,pnbc,pndc->pad", over_part, nearby, fock_part, precision=HIGH)
    second = jnp.einsum("pnab,pnbc,pndc->pad", fock_part, nearby, over_part, precision=HIGH)
    return first + second


def solution(mesh):
    placed = (
        P("row", "col"),
        P("row", "col"),
        P(None, "row", "col"),
        P(("row", "col"), None, None, None),
        P(("row", "col"), None),
        P(("row", "col"), None),
        P(("row", "col"), None, None),
    )
    return jax.shard_map(
        shards, mesh=mesh, in_specs=placed, out_specs=P(("row", "col"), None, None), check_vma=False
    )
```

time: 1150 us -> 262 us (0.23); the launches traced: 1140 us -> 262 us
  local copies, waits for them, and re-layouts: 564 us -> 15 us
  other arithmetic: 215 us -> 4.14 us
  matrix products: 144 us -> 0.95 us
  waiting for transfers between devices: 48.2 us -> 14.6 us
  Pallas kernels: 0 us -> 29.2 us
  blocking collectives: 140 us -> 169 us
    gather x68 -> x2, local copies, waits for them, and re-layouts: 417 us -> 3.63 us  [shards(): linked = jnp.take(coln, nb.reshape(-1), axis=0).reshape(pairs, 2)]
    convert_element_type x16 -> x0, other arithmetic: 152 us -> none  [the longest x8 151 us: one_group(): left = total.astype(jnp.bfloat16)]
    dot_general x24 -> x0, matrix products: 143 us -> none  [the longest x8 70.9 us: one_group(): jnp.einsum('tmak,tkw->tmaw', blocks, operator, preferred_element_type=jnp...]
    all_gather x2 -> x1, waiting for transfers between devices: 45.8 us -> 8.75 us  [shards(): lax.all_gather(coefficients.reshape(pair_dev * slots, rows, tile), both,...]
    reshape x10 -> x6, local copies, waits for them, and re-layouts: 39 us -> 6.38 us  [the longest x1 3.9 us: shards(): g = g.reshape(lax.axis_size('row'), lax.axis_size('col'), 2, 24, 128)]
    pallas_call x0 -> x1, Pallas kernels: none -> 29.2 us  [shards(): pl.pallas_call(functools.partial(pair_blocks_kernel, (pairs, slots, rows,...]
    all_gather x4 -> x2, blocking collectives: 140 us -> 169 us  [the longest x1 109 us: shards(): every_amp = lax.all_gather(amplitudes, both, axis=0, tiled=True)]
    another operation x2 -> x0, local copies, waits for them, and re-layouts: 23.2 us -> none  [the longest x1 13.8 us: bucket_slots(): flat_coeffs = coeffs.reshape((slot_count,) + coeffs.shape[2:])]
  transfers between devices with their start and end apart: 4 -> 3, of which waited for: 2 -> 2; matrix products, arithmetic and copies ran while one was open for 6% -> 5% of each run, Pallas kernels for 0% -> 0%
where the time goes in v1:
time: 262 us
  blocking collectives  169 us (65%)
  Pallas kernels  29.2 us (11%)
  starting transfers between devices  15.4 us (6%)
  local copies, waits for them, and re-layouts  15 us (6%)
  waiting for transfers between devices  14.6 us (6%)
  between operations  13.5 us (5%)
  other arithmetic  4.14 us (2%)
    all_gather x1, blocking collectives, shards(): every_amp = lax.all_gather(amplitudes, both, axis=0, tiled=True)  109 us
    all_gather x1, blocking collectives, shards(): lax.all_gather(jnp.concatenate([domains, neighbours], axis=1), both, axis...  59.4 us
    pallas_call x1, Pallas kernels, shards(): pl.pallas_call(functools.partial(pair_blocks_kernel, (pairs, slots, rows,...  29.2 us
    all_to_all x1, starting transfers between devices, shards(): lax.all_to_all(g, 'col', split_axis=1, concat_axis=1, tiled=True)  10.4 us
    all_gather x1, waiting for transfers between devices, shards(): lax.all_gather(coefficients.reshape(pair_dev * slots, rows, tile), both,...  8.75 us
    all_to_all x1, waiting for transfers between devices, shards(): lax.all_to_all(g, 'row', split_axis=0, concat_axis=0, tiled=True)  5.85 us
  transfers between devices with their start and end apart: 3, of which 2 were waited for; matrix products, arithmetic and copies ran while one was open for 5% of the time, Pallas kernels for 0%

profile of v1, /device:TPU:1, one launch (start us, length us, event | category | flops | bytes accessed | tf_op | source)
XLA Modules:
  0.0 261.8 jit_solution(6664748188479320215)
XLA Ops:
  6.5 0.0 copy-start.1
  6.5 0.0 all-gather.3.cloned.1.call-start
  6.5 1.5 copy.29
  8.1 0.0 all-gather.3.cloned.1.call-update
  8.1 0.8 add_bitcast_fusion
  8.9 59.4 %all-gather = s32[128,2,9]{2,1,0:T(2,128)S(1)} all-gather(s32[1,2,9]{2,1,0:T(2,128)S(1)} %add_bitcast_fusion), channel_id=1, replica_groups=mesh['row'=8,'col'=16] {'row','col'}, dimensions={0}, use_global_device_ids=true | all-gather | bytes 9288 | tf_op jit(solution)/shard_map/all_gather | solution.py:125
  68.3 0.1 slice.92
  68.4 0.1 reshape.152
  68.6 0.7 reshape.151.nb
  69.3 0.7 compare_and_fusion
  70.0 0.2 add_reduce_fusion
  70.2 0.6 convert_add_fusion
  70.8 3.5 %gather_fusion.1 = s32[512]{0:T(512)S(1)} fusion(s32[256]{0:T(256)S(1)} %get-tuple-element.41, s32[1024]{0:T(1024)S(1)} %pad_clamp_fusion), kind=kCustom, calls=%fused_computation.1 | custom fusion | bytes 6144 | tf_op jit(solution)/shard_map/jit(_take)/gather | solution.py:129
  74.3 0.1 gather.12
  74.5 0.8 reshape.150.dom
  75.3 0.0 copy-done.1
  75.3 0.1 copy.28
  75.4 0.7 reshape.153.mask
  76.1 0.2 fusion.13
  76.2 0.2 fusion.2
  76.4 0.6 and_select_fusion.1
  77.0 8.7 %all-gather.3.cloned.1.call-done.c_hbm = bf16[1792,20,128]{2,1,0:T(8,128)(2,1)} async-done(((bf16[14,20,128]{2,1,0:T(8,128)(2,1)}), bf16[1792,20,128]{2,1,0:T(8,128)(2,1)}) %all-gather.3.cloned.1.call-update) | async-done | bytes 9175056 | tf_op jit(solution)/shard_map/all_gather | solution.py:124
  85.8 29.2 %shard_map.73 = f32[256,24,128]{2,1,0:T(8,128)} custom-call(s32[1792]{0:T(1024)} %reshape.150.dom, s32[512]{0:T(512)} %reshape.151.nb, s32[256]{0:T(256)} %get-tuple-element.40.rowp, s32[256]{0:T(256)} %get-tuple-element.42.colp, s32[256]{0:T(256)} %get-tuple-element.39.work, s32[324]{0:T(512)} %reshape.153.mask, ...), custom_call_target="tpu_custom_call" | custom-call | tf_op jit(solution)/shard_map/pallas_call | solution.py:135
  115.0 3.9 %copy.30 = f32[8,16,2,24,128]{4,3,2,0,1:T(8,128)} copy(f32[8,16,2,24,128]{4,3,2,1,0:T(8,128)} %bitcast.35) | data formatting | bytes 6291456 | tf_op jit(solution)/shard_map/reshape | solution.py:150
  118.9 0.0 copy-start
  118.9 0.0 copy-start.2
  118.9 10.4 %all-to-all-start = ((f32[8,16,2,24,128]{4,3,2,0,1:T(8,128)}), f32[8,16,2,24,128]{4,3,2,0,1:T(8,128)S(1)}, u32[]{:S(2)}, u32[]{:S(2)}) async-start(f32[8,16,2,24,128]{4,3,2,0,1:T(8,128)} %copy.30), calls=%async_computation | async-start | bytes 6291456 | tf_op jit(solution)/shard_map/all_to_all | solution.py:151
  129.4 0.0 copy-done
  129.4 0.0 copy-done.2
  129.4 0.1 reshape.169
  129.5 109.4 %all_gather.9 = f32[256,20,20]{2,1,0:T(8,128)} all-gather(f32[2,20,20]{2,1,0:T(8,128)S(1)} %copy.26), channel_id=1, replica_groups=mesh['row'=8,'col'=16] {'row','col'}, dimensions={0}, use_global_device_ids=true | all-gather | bytes 412800 | tf_op jit(solution)/shard_map/all_gather | solution.py:156
  239.0 2.4 gather_fusion
  241.4 0.1 copy.27
  241.5 0.0 all-to-all-done
  241.5 0.8 reduce_sum.28
  242.4 4.9 %all-to-all-start.1 = ((f32[8,2,24,128]{3,2,1,0:T(8,128)}), f32[8,2,24,128]{3,2,1,0:T(8,128)S(1)}, u32[]{:S(2)}, u32[]{:S(2)}) async-start(f32[8,2,24,128]{3,2,1,0:T(8,128)} %reduce_sum.28), calls=%async_computation.1 | async-start | bytes 393216 | tf_op jit(solution)/shard_map/all_to_all | solution.py:152
  247.3 5.8 %all-to-all-done.1 = f32[8,2,24,128]{3,2,1,0:T(8,128)S(1)} async-done(((f32[8,2,24,128]{3,2,1,0:T(8,128)}), f32[8,2,24,128]{3,2,1,0:T(8,128)S(1)}, u32[]{:S(2)}, u32[]{:S(2)}) %all-to-all-start.1) | async-done | bytes 196640 | tf_op jit(solution)/shard_map/all_to_all | solution.py:152
  253.2 0.1 reshape.189
  253.3 0.3 fusion.3
  253.6 0.3 fusion.4
  253.9 0.2 convolution_bitcast_fusion
  254.1 0.2 fusion
  254.3 0.6 copy.36
  (8 shorter events, 0.1 us)
Async XLA Ops:
  6.5 68.7 %copy-start.1 = (s32[2,18,9]{1,0,2:T(2,128)S(1)}, s32[2,18,9]{1,0,2:T(2,128)}, u32[]{:S(2)}) copy-start(s32[2,18,9]{1,0,2:T(2,128)} %param.9) | copy-start | bytes 3892
  6.5 79.2 %all-gather.3.cloned.1.call-start = ((), (), s32[]{:S(2)}) async-start(), calls=%async_computation.2 | async-start | bytes 11096064 | tf_op jit(solution)/shard_map/all_gather | solution.py:124
  118.9 10.4 %copy-start = (f32[2,20,20]{2,0,1:T(2,128)S(1)}, f32[2,20,20]{2,0,1:T(2,128)}, u32[]{:S(2)}) copy-start(f32[2,20,20]{2,0,1:T(2,128)} %param.13) | copy-start | bytes 9604
  118.9 10.5 %copy-start.2 = (s32[2,2]{1,0:T(2,128)S(1)}, s32[2,2]{1,0:T(2,128)}, u32[]{:S(2)}) copy-start(s32[2,2]{1,0:T(2,128)} %param.12) | copy-start | bytes 52
  118.9 122.6 %all-to-all-start = ((f32[8,16,2,24,128]{4,3,2,0,1:T(8,128)}), f32[8,16,2,24,128]{4,3,2,0,1:T(8,128)S(1)}, u32[]{:S(2)}, u32[]{:S(2)}) async-start(f32[8,16,2,24,128]{4,3,2,0,1:T(8,128)} %copy.30), calls=%async_computation | async-start | bytes 6291456 | tf_op jit(solution)/shard_map/all_to_all | solution.py:151
  242.4 10.8 %all-to-all-start.1 = ((f32[8,2,24,128]{3,2,1,0:T(8,128)}), f32[8,2,24,128]{3,2,1,0:T(8,128)S(1)}, u32[]{:S(2)}, u32[]{:S(2)}) async-start(f32[8,2,24,128]{3,2,1,0:T(8,128)} %reduce_sum.28), calls=%async_computation.1 | async-start | bytes 393216 | tf_op jit(solution)/shard_map/all_to_all | solution.py:152
Sparse Core Ops, SparseCore 0:
  10.4 75.3 all-gather.2

commit v2 on v1

--- a/solution.py
+++ b/solution.py
@@ -1,6 +1,7 @@
 import functools
 import jax
 import jax.numpy as jnp
+import numpy as np
 from jax import lax
 from jax.experimental import pallas as pl
 from jax.experimental.pallas import tpu as pltpu
@@ -9,6 +10,249 @@
 HIGH = lax.Precision.HIGHEST
 UNROLL = 4
 LANES = 32
+MESH = pl.DeviceIdType.MESH
+SIDE = 4
+SHARES = ((0, 5), (5, 5), (10, 4))
+ORDERS = ("xyz", "yzx", "zxy")
+
+
+def chip_place():
+    row, col = lax.axis_index("row"), lax.axis_index("col")
+    return {"z": lax.div(row, 2), "y": lax.div(col, SIDE), "x": lax.rem(col, SIDE)}, lax.rem(row, 2)
+
+
+def device_at(place, core):
+    return (place["z"] * 2 + core, place["y"] * SIDE + place["x"])
+
+
+def moved(place, axis, step):
+    return {**place, axis: lax.rem(place[axis] + step + SIDE, SIDE)}
+
+
+def slot_address(pairs, slots):
+    p, s = np.divmod(np.arange(pairs * slots), slots)
+    device, within = p // 2, (p % 2) * slots + s
+    row, col = device // 16, device % 16
+    at = {"z": row // 2, "y": col // SIDE, "x": col % SIDE}
+    out = np.zeros(pairs * slots, np.int32)
+    for (first, count), order in zip(SHARES, ORDERS):
+        a, b, c = (at[axis] for axis in order)
+        place = (((row % 2) * SIDE + c) * SIDE + b) * SIDE + a
+        mine = (within >= first) & (within < first + count)
+        out[mine] = (first * (pairs // 2) + place * count + within - first)[mine]
+    return out
+
+
+def gather_kernel(own, meta, o0, o1, o2, om, send, recv, local):
+    place, core = chip_place()
+    barrier = pltpu.get_barrier_semaphore()
+    peers = [device_at(moved(place, axis, step), core) for axis in "xyz" for step in (1, -1)]
+    peers.append(device_at(place, 1 - core))
+    for peer in peers:
+        pl.semaphore_signal(barrier, inc=1, device_id=peer, device_id_type=MESH)
+    pl.semaphore_wait(barrier, len(peers))
+    started = []
+
+    def push(src, dst, peer):
+        i = len(started)
+        copy = pltpu.make_async_remote_copy(
+            src_ref=src, dst_ref=dst, send_sem=send.at[i], recv_sem=recv.at[i], device_id=peer, device_id_type=MESH
+        )
+        copy.start()
+        started.append(copy)
+        return copy
+
+    def index(axis, step):
+        return lax.rem(place[axis] + step + SIDE, SIDE)
+
+    plans = []
+    for k, (out, order) in enumerate(zip((o0, o1, o2, om), ORDERS + ORDERS[2:])):
+        if k < 3:
+            src = own.at[pl.ds(*SHARES[k])]
+            half = SHARES[k][1] // 2
+            parts = (pl.ds(0, half), pl.ds(half, SHARES[k][1] - half))
+        else:
+            src, parts = meta, (None, None)
+        plans.append((k, out.at[core], out, order, src, parts))
+
+    keep, state = [], [dict() for _ in plans]
+    for k, out, _, (a, b, c), src, _ in plans:
+        here = out.at[index(c, 0), index(b, 0), index(a, 0)]
+        state[k]["a"] = [push(src, here, device_at(moved(place, a, step), core)) for step in (1, -1)]
+        copy = pltpu.make_async_copy(src, here, local.at[k])
+        copy.start()
+        keep.append(copy)
+    for k, out, _, (a, b, c), _, parts in plans:
+        later = []
+        for step, copy, part in zip((1, -1), state[k]["a"], parts):
+            copy.wait_recv()
+            if part is None:
+                if step == 1:
+                    block = out.at[index(c, 0), index(b, 0), index(a, -1)]
+                    later.append(push(block, block, device_at(moved(place, a, 1), core)))
+                continue
+            block = out.at[index(c, 0), index(b, 0), index(a, -step), part]
+            later.append(push(block, block, device_at(moved(place, a, step), core)))
+        state[k]["aa"] = later
+
+    def line(out, axes, j):
+        return out.at[index(axes[2], 0), index(axes[1], j)]
+
+    def spread(k, j):
+        _, out, _, axes, _, _ = plans[k]
+        block = line(out, axes, j)
+        state[k]["c%d" % j] = [push(block, block, device_at(moved(place, axes[2], step), core)) for step in (1, -1)]
+
+    def pass_on(k, j):
+        _, out, _, (a, b, c), _, _ = plans[k]
+        later = []
+        for step, copy in zip((1, -1), state[k]["c%d" % j]):
+            copy.wait_recv()
+            part = pl.ds(0, 2) if step == 1 else pl.ds(2, 2)
+            block = out.at[index(c, -step), index(b, j), part]
+            later.append(push(block, block, device_at(moved(place, c, step), core)))
+        state[k]["cc%d" % j] = later
+
+    def share(k, step):
+        _, out, _, (a, b, c), _, _ = plans[k]
+        block = out.at[index(c, step)]
+        state[k].setdefault("share", []).append(push(block, block, device_at(place, 1 - core)))
+
+    for k, out, _, (a, b, c), _, _ in plans:
+        for copy in state[k]["aa"]:
+            copy.wait_recv()
+        keep[k].wait()
+        block = line(out, (a, b, c), 0)
+        state[k]["b"] = [push(block, block, device_at(moved(place, b, step), core)) for step in (1, -1)]
+        spread(k, 0)
+    for k, out, _, (a, b, c), _, _ in plans:
+        later = []
+        for step, copy in zip((1, -1), state[k]["b"]):
+            copy.wait_recv()
+            part = pl.ds(0, 2) if step == 1 else pl.ds(2, 2)
+            block = out.at[index(c, 0), index(b, -step), part]
+            later.append(push(block, block, device_at(moved(place, b, step), core)))
+            spread(k, -step)
+        state[k]["bb"] = later
+    for k in range(4):
+        pass_on(k, 0)
+    for k in range(4):
+        for copy in state[k]["bb"]:
+            copy.wait_recv()
+        spread(k, 2)
+        share(k, 0)
+    for j in (-1, 1, 2):
+        for k in range(4):
+            pass_on(k, j)
+    for k in range(4):
+        share(k, -1)
+        share(k, 1)
+    for k in range(4):
+        for j in (0, -1, 1, 2):
+            for copy in state[k]["cc%d" % j]:
+                copy.wait_recv()
+        share(k, 2)
+    for k in range(4):
+        for copy in state[k]["share"]:
+            copy.wait_recv()
+    for copy in started:
+        copy.wait_send()
+
+
+def gather_all(coefficients, meta):
+    count, rows, tile = coefficients.shape
+    cube = (2, SIDE, SIDE, SIDE)
+    shapes = [jax.ShapeDtypeStruct(cube + (n, rows, tile), coefficients.dtype) for _, n in SHARES]
+    shapes.append(jax.ShapeDtypeStruct(cube + meta.shape, meta.dtype))
+    copies = 3 * 28 + 27
+    return pl.pallas_call(
+        gather_kernel,
+        name="gather",
+        out_shape=shapes,
+        in_specs=[pl.BlockSpec(memory_space=pltpu.VMEM)] * 2,
+        out_specs=[pl.BlockSpec(memory_space=pl.ANY)] * 4,
+        scratch_shapes=[
+            pltpu.SemaphoreType.DMA((copies,)),
+            pltpu.SemaphoreType.DMA((copies,)),
+            pltpu.SemaphoreType.DMA((4,)),
+        ],
+        compiler_params=pltpu.CompilerParams(collective_id=0, has_side_effects=True),
+    )(coefficients, meta)
+
+
+def reduce_kernel(g, out, other, mine, arrived, sems, send, recv):
+    place, core = chip_place()
+    steps = [(dz, dy, dx) for dz in range(SIDE) for dy in range(SIDE) for dx in range(SIDE)]
+    barrier = pltpu.get_barrier_semaphore()
+    partner = device_at(place, 1 - core)
+
+    def chip(dz, dy, dx):
+        return moved(moved(moved(place, "z", dz), "y", dy), "x", dx)
+
+    def blocks_of(at):
+        return pl.ds(2 * ((at["z"] * SIDE + at["y"]) * SIDE + at["x"]), 2)
+
+    peers = [device_at(chip(*d), core) for d in steps[1:]] + [partner]
+    for peer in peers:
+        pl.semaphore_signal(barrier, inc=1, device_id=peer, device_id_type=MESH)
+    pl.semaphore_wait(barrier, len(peers))
+    plane = 2 * SIDE * SIDE
+    swaps = []
+    for d in range(SIDE):
+        part = pl.ds(lax.rem(place["z"] + d + 1, SIDE) * plane, plane)
+        swaps.append(
+            pltpu.make_async_remote_copy(
+                src_ref=g.at[1 - core, part], dst_ref=other.at[part], send_sem=sems.at[0, d],
+                recv_sem=sems.at[1, d], device_id=partner, device_id_type=MESH,
+            )
+        )
+        swaps[-1].start()
+    copies = []
+    for d in range(SIDE):
+        swaps[d].wait_recv()
+        part = pl.ds(lax.rem(place["z"] + d + 1, SIDE) * plane, plane)
+        mine[part] = (g[core, part] + other[part]).astype(mine.dtype)
+        for i, step in enumerate(steps):
+            if step[0] == (d + 1) % SIDE and i > 0:
+                at = chip(*step)
+                copy = pltpu.make_async_remote_copy(
+                    src_ref=mine.at[blocks_of(at)], dst_ref=arrived.at[i], send_sem=send.at[i],
+                    recv_sem=recv.at[i], device_id=device_at(at, core), device_id_type=MESH,
+                )
+                copy.start()
+                copies.append((i, copy))
+    own = blocks_of(place)
+    total = g[core, own] + other[own]
+    for i, copy in copies:
+        copy.wait_recv()
+        total = total + arrived[i].astype(jnp.float32)
+    out[...] = total
+    for copy in swaps:
+        copy.wait_send()
+    for _, copy in copies:
+        copy.wait_send()
+
+
+def reduce_all(g):
+    _, blocks, rows, lanes = g.shape
+    chips = blocks // 2
+    vmem = pl.BlockSpec(memory_space=pltpu.VMEM)
+    return pl.pallas_call(
+        reduce_kernel,
+        name="reduce",
+        out_shape=jax.ShapeDtypeStruct((2, rows, lanes), jnp.float32),
+        in_specs=[vmem],
+        out_specs=vmem,
+        scratch_shapes=[
+            pltpu.VMEM((blocks, rows, lanes), jnp.float32),
+            pltpu.VMEM((blocks, rows, lanes), jnp.bfloat16),
+            pltpu.VMEM((chips, 2, rows, lanes), jnp.bfloat16),
+            pltpu.SemaphoreType.DMA((2, SIDE)),
+            pltpu.SemaphoreType.DMA((chips,)),
+            pltpu.SemaphoreType.DMA((chips,)),
+        ],
+        compiler_params=pltpu.CompilerParams(collective_id=1, has_side_effects=True, vmem_limit_bytes=40 * 2**20),
+    )(g)
 
 
 def slot_tables(tiles, first, count):
@@ -22,13 +266,15 @@
 
 
 def pair_blocks_kernel(
-    dims, dom, nb, rowp, colp, work, mask, c_hbm, f_hbm, s_hbm, g_ref, cv, fv, sv, l1, l2, sems
+    dims, dom, address, nb, rowp, colp, work, mask, c0, c1, c2, f_hbm, s_hbm, g_ref, cv, fv, sv, l1, l2, sems
 ):
     pairs, slots, rows, tile, tile_rows, tile_cols = dims
     copies = (
-        pltpu.make_async_copy(c_hbm, cv, sems.at[0]),
-        pltpu.make_async_copy(f_hbm, fv, sems.at[1]),
-        pltpu.make_async_copy(s_hbm, sv, sems.at[2]),
+        pltpu.make_async_copy(f_hbm, fv, sems.at[0]),
+        pltpu.make_async_copy(s_hbm, sv, sems.at[1]),
+    ) + tuple(
+        pltpu.make_async_copy(c, cv.at[pl.ds(first * (pairs // 2), n * (pairs // 2))], sems.at[2 + i])
+        for i, (c, (first, n)) in enumerate(zip((c0, c1, c2), SHARES))
     )
     for c in copies:
         c.start()
@@ -40,6 +286,9 @@
     def one_pair(d, i, counts):
         p = 2 * d + i
         w = work[p]
+
+        row, col = lax.div(d, 16), lax.rem(d, 16)
+        spot = lax.rem(row, 2) * 64 + lax.div(row, 2) * 16 + col
 
         def busy(counts):
             out = list(counts)
@@ -54,6 +303,7 @@
                 def by_row(x, cnt, k=k, packed_cols=packed_cols, n_cols=n_cols, q=q):
                     sa = p * slots + ((packed_rows >> (3 * x)) & 7)
                     a = dom[sa] - row0
+                    from_a = address[sa]
 
                     def by_col(y, cnt):
                         sb = k * slots + ((packed_cols >> (3 * y)) & 7)
@@ -61,8 +311,8 @@
                         cell = a * tile_cols + b
                         m0 = mask[cell]
                         m1 = mask[cells + cell]
-                        l1[q, cnt] = sa | (sb << 11) | (a << 22) | (b << 27)
-                        l2[q, cnt] = d | (m0 << 8) | (m1 << 9)
+                        l1[q, cnt] = from_a | (address[sb] << 11) | (a << 22) | (b << 27)
+                        l2[q, cnt] = spot | (m0 << 8) | (m1 << 9)
                         return cnt + (m0 | m1)
 
                     return lax.fori_loop(0, n_cols, by_col, cnt)
@@ -121,9 +371,13 @@
     n_dev = lax.axis_size("row") * lax.axis_size("col")
     pairs = pair_dev * n_dev
     both = ("row", "col")
-    c_all = lax.all_gather(coefficients.reshape(pair_dev * slots, rows, tile), both, axis=0, tiled=True)
-    tabs = lax.all_gather(jnp.concatenate([domains, neighbours], axis=1), both, axis=0, tiled=True)
-    dom, nb = tabs[:, :slots], tabs[:, slots:]
+    amps = jnp.pad(amplitudes.reshape(-1), (0, 7 * 128 - amplitudes.size)).reshape(7, 128)
+    names = jnp.concatenate([domains.reshape(-1), neighbours.reshape(-1)]).astype(jnp.float32)
+    meta = jnp.concatenate([amps, jnp.pad(names, (0, 128 - names.size)).reshape(1, 128)])
+    c0, c1, c2, metas = gather_all(coefficients.reshape(pair_dev * slots, rows, tile), meta)
+    metas = metas.transpose(3, 0, 1, 2, 4, 5).reshape(n_dev, 8, 128)
+    ints = metas[:, 7, : names.size].astype(jnp.int32)
+    dom, nb = ints[:, : domains.size].reshape(pairs, slots), ints[:, domains.size :].reshape(pairs, 2)
     rowp, rown = slot_tables(dom, lax.axis_index("row") * tile_rows, tile_rows)
     colp, coln = slot_tables(dom, lax.axis_index("col") * tile_cols, tile_cols)
     linked = jnp.take(coln, nb.reshape(-1), axis=0).reshape(pairs, 2)
@@ -131,11 +385,11 @@
     work = jnp.where((rown > 0) & (linked.sum(axis=1) > 0), work, 0)
     smem = pl.BlockSpec(memory_space=pltpu.SMEM)
     anys = pl.BlockSpec(memory_space=pl.ANY)
-    cap = tile_rows * 2 * (pairs // 32) // 2 * slots + 2 * UNROLL
     g = pl.pallas_call(
         functools.partial(pair_blocks_kernel, (pairs, slots, rows, tile, tile_rows, tile_cols)),
         out_shape=jax.ShapeDtypeStruct((2 * n_dev, 24, 128), jnp.float32),
-        in_specs=[smem] * 6 + [anys] * 3,
+        name="pairs",
+        in_specs=[smem] * 7 + [anys] * 5,
         out_specs=pl.BlockSpec(memory_space=pltpu.VMEM),
         scratch_shapes=[
             pltpu.VMEM((pairs * slots, rows, tile), jnp.bfloat16),
@@ -143,18 +397,21 @@
             pltpu.VMEM(fock.shape, jnp.bfloat16),
             pltpu.SMEM((4, 2048), jnp.int32),
             pltpu.SMEM((4, 2048), jnp.int32),
-            pltpu.SemaphoreType.DMA((3,)),
+            pltpu.SemaphoreType.DMA((5,)),
         ],
         compiler_params=pltpu.CompilerParams(vmem_limit_bytes=56 * 2**20),
-    )(dom.reshape(-1), nb.reshape(-1), rowp, colp, work, tile_mask.reshape(-1), c_all, fock, intersection)
-    g = g.reshape(lax.axis_size("row"), lax.axis_size("col"), 2, 24, 128)
-    g = lax.all_to_all(g, "col", split_axis=1, concat_axis=1, tiled=True).sum(axis=1)
-    g = lax.all_to_all(g, "row", split_axis=0, concat_axis=0, tiled=True).sum(axis=0)
+    )(
+        dom.reshape(-1), jnp.asarray(slot_address(pairs, slots)), nb.reshape(-1), rowp, colp, work,
+        tile_mask.reshape(-1), *(c.reshape(-1, rows, tile) for c in (c0, c1, c2)), fock, intersection,
+    )
+    g = reduce_all(g.reshape(2, n_dev, 24, 128))
     blocks = g[:, :rows].reshape(2, rows, 2, 2, LANES)[..., :rows]
     fock_part = jnp.transpose(blocks[0], (1, 2, 0, 3))
     over_part = jnp.transpose(blocks[1], (1, 2, 0, 3))
-    every_amp = lax.all_gather(amplitudes, both, axis=0, tiled=True)
-    nearby = jnp.take(every_amp, neighbours, axis=0)
+    picked = jnp.take(metas[:, :7], neighbours.reshape(-1) // 2, axis=0).reshape(4, -1)[:, : amplitudes.size]
+    picked = picked.reshape(4, 2, rows, rows)
+    odd = (neighbours.reshape(4, 1, 1) % 2) == 1
+    nearby = jnp.where(odd, picked[:, 1], picked[:, 0]).reshape(2, 2, rows, rows)
     first = jnp.einsum("pnab,pnbc,pndc->pad", over_part, nearby, fock_part, precision=HIGH)
     second = jnp.einsum("pnab,pnbc,pndc->pad", fock_part, nearby, over_part, precision=HIGH)
     return first + second

time: 262 us -> 123 us (0.47)
  blocking collectives: 169 us -> 0 us
  Pallas kernels: 29.2 us -> 103 us
  starting transfers between devices: 15.4 us -> 0 us
  waiting for transfers between devices: 14.6 us -> 0 us
  between operations: 13.5 us -> 0.19 us
    all_gather x2 -> x0, blocking collectives: 169 us -> none  [the longest x1 109 us: shards(): every_amp = lax.all_gather(amplitudes, both, axis=0, tiled=True)]
    pallas_call x0 -> x2, Pallas kernels: none -> 67.1 us  [the longest x1 46.1 us: gather_all(): pl.pallas_call(gather_kernel, name='gather', out_shape=shapes, in_specs=[...]
    all_to_all x2 -> x0, starting transfers between devices: 15.4 us -> none  [the longest x1 10.4 us: shards(): lax.all_to_all(g, 'col', split_axis=1, concat_axis=1, tiled=True)]
    all_gather x1 -> x0, waiting for transfers between devices: 8.75 us -> none  [shards(): lax.all_gather(coefficients.reshape(pair_dev * slots, rows, tile), both,...]
    pallas_call x1, Pallas kernels: 29.2 us -> 35.5 us  [shards(): pl.pallas_call(functools.partial(pair_blocks_kernel, (pairs, slots, rows,...]
    all_to_all x2 -> x0, waiting for transfers between devices: 5.85 us -> none  [the longest x1 5.85 us: shards(): lax.all_to_all(g, 'row', split_axis=0, concat_axis=0, tiled=True)]
    unnamed x9 -> x6, local copies, waits for them, and re-layouts: 1.65 us -> 4.94 us
    reshape x4 -> x8, local copies, waits for them, and re-layouts: 5.58 us -> 2.57 us  [the longest x2 1.52 us: shards(): neighbours.reshape(-1) // 2]
  transfers between devices with their start and end apart: 3 -> 0, of which waited for: 2 -> 0; matrix products, arithmetic and copies ran while one was open for 5% -> 0% of each run, Pallas kernels for 0% -> 0%
where the time goes in v2:
time: 123 us; the launch traced here: 124 us
  Pallas kernels  103 us (84%)
  local copies, waits for them, and re-layouts  15.9 us (13%)
  other arithmetic  3.97 us (3%)
    pallas_call x1, Pallas kernels, gather_all(): pl.pallas_call(gather_kernel, name='gather', out_shape=shapes, in_specs=[...  46.1 us
    pallas_call x1, Pallas kernels, shards(): pl.pallas_call(functools.partial(pair_blocks_kernel, (pairs, slots, rows,...  35.5 us
    pallas_call x1, Pallas kernels, reduce_all(): pl.pallas_call(reduce_kernel, name='reduce', out_shape=jax.ShapeDtypeStru...  21 us
    unnamed x6, local copies, waits for them, and re-layouts  4.94 us
    gather x2, local copies, waits for them, and re-layouts, shards(): linked = jnp.take(coln, nb.reshape(-1), axis=0).reshape(pairs, 2)  3.63 us

profile of v2, /device:TPU:1, one launch (start us, length us, event | category | flops | bytes accessed | tf_op | source)
XLA Modules:
  0.0 123.6 jit_solution(11757152580979625445)
XLA Ops:
  0.0 0.7 fusion.6
  0.7 0.8 reshape.294
  1.5 0.8 reshape.298
  2.2 0.1 add_convert_fusion
  2.3 0.8 reshape.301
  3.1 0.8 copy.16
  3.9 0.7 reshape.304.mask
  4.6 0.7 copy.14
  5.3 0.1 reshape.296
  5.4 0.6 pad_maximum_fusion.meta
  6.0 1.5 %copy.13 = bf16[2,7,20,128]{3,2,1,0:T(8,128)(2,1)} copy(bf16[2,7,20,128]{3,0,2,1:T(2,128)(2,1)} %param.11) | data formatting | bytes 143360 | tf_op args[3]
  7.6 46.1 %gather.21 = (bf16[2,4,4,4,5,20,128]{6,5,4,3,2,1,0:T(8,128)(2,1)}, bf16[2,4,4,4,5,20,128]{6,5,4,3,2,1,0:T(8,128)(2,1)}, bf16[2,4,4,4,4,20,128]{6,5,4,3,2,1,0:T(8,128)(2,1)}, f32[2,4,4,4,8,128]{5,4,3,2,1,0:T(8,128)}) custom-call(bf16[14,20,128]{2,1,0:T(8,128)(2,1)} %bitcast.75, f32[8,128]{1,0:T(8,128)} %pad_maximum_fusion.meta), custom_call_target="tpu_custom_call" | custom-call | tf_op jit(solution)/shard_map/gather/pallas_call | solution.py:168
  53.7 1.1 copy.15
  54.8 0.6 gather_fusion
  55.3 0.1 slice_select_fusion
  55.4 0.1 slice_convert_fusion
  55.5 0.7 reshape_reshape.11.dom
  56.2 0.1 slice.110
  56.3 0.1 reshape_reshape.14
  56.4 0.7 reshape_reshape.12.nb
  57.1 0.1 reshape_reshape.13
  57.2 0.1 reshape.302
  57.3 0.1 reshape.303
  57.4 0.7 compare_and_fusion
  58.1 0.2 add_reduce_fusion
  58.3 0.6 convert_add_fusion
  58.9 3.5 %gather_fusion.1 = s32[512]{0:T(512)S(1)} fusion(s32[256]{0:T(256)S(1)} %get-tuple-element.51, s32[1024]{0:T(1024)S(1)} %pad_clamp_fusion), kind=kCustom, calls=%fused_computation.1 | custom fusion | bytes 6144 | tf_op jit(solution)/shard_map/jit(_take)/gather | solution.py:383
  62.4 0.1 gather.16
  62.6 0.1 fusion.8
  62.7 0.2 fusion.2
  62.9 0.6 and_select_fusion.1
  63.5 35.5 %pairs.1 = f32[256,24,128]{2,1,0:T(8,128)} custom-call(s32[1792]{0:T(1024)} %reshape_reshape.11.dom, s32[1792]{0:T(1024)} %constant.103.clone.address, s32[512]{0:T(512)} %reshape_reshape.12.nb, s32[256]{0:T(256)} %get-tuple-element.50.rowp, s32[256]{0:T(256)} %get-tuple-element.52.colp, s32[256]{0:T(256)} %get-tuple-element.49.work, s32[324]{0:T(512)} %reshape.304.mask, ...), custom_call_target="tpu_custom_call" | custom-call | tf_op jit(solution)/shard_map/pairs/pallas_call | solution.py:388
  98.9 0.0 copy-start
  99.0 1.9 %copy-done = f32[256,24,128]{2,1,0:T(8,128)S(1)} copy-done((f32[256,24,128]{2,1,0:T(8,128)S(1)}, f32[256,24,128]{2,1,0:T(8,128)}, u32[]{:S(2)}) %copy-start) | copy-done | bytes 3145752
  100.8 21.0 %reduce.33 = f32[2,24,128]{2,1,0:T(8,128)S(1)} custom-call(f32[2,128,24,128]{3,2,1,0:T(8,128)S(1)} %bitcast.60), custom_call_target="tpu_custom_call" | custom-call | tf_op jit(solution)/shard_map/reduce/pallas_call | solution.py:240
  121.8 0.1 reshape.338
  122.0 0.3 fusion.4
  122.3 0.3 fusion.3
  122.6 0.2 convolution_bitcast_fusion
  122.8 0.2 fusion
  122.9 0.6 copy.20
  (10 shorter events, 0.1 us)
Async XLA Ops:
  98.9 1.9 %copy-start = (f32[256,24,128]{2,1,0:T(8,128)S(1)}, f32[256,24,128]{2,1,0:T(8,128)}, u32[]{:S(2)}) copy-start(f32[256,24,128]{2,1,0:T(8,128)} %pairs.1) | copy-start | bytes 9437188
